TPU v7x, 512 devices: a whole 4x4x16 slice. The times are simulated.
512 devices in a mesh: tm: 8 (over x, core), dp: 64 (over z, y).
Axes of the slice: x: 4, y: 4, z: 16, core: 2. Of those that a mesh axis runs over, the one named last changes fastest.
Arguments:
- edge_feat: bfloat16 [8, 8192, 186], P('tm', 'dp'), may hold values from -6 to 6
- endpoint_slots: int32 [8, 2, 8192], P('tm', None, 'dp'), may hold values from 0 to 2047, as said below
- neighbor_slots: int32 [8, 20, 8192], P('tm', None, 'dp'), may hold values from 0 to 2047, as said below
- neighbor_gap: int32 [8, 20, 8192], P('tm', None, 'dp'), may hold values from 0 to 999
- score_grad: float32 [8, 8192], P('tm', 'dp'), may hold values from -1.5 to 1.5
- node_list: int32 [8, 64, 2048], P('tm', 'dp'), may hold values from 0 to 128, as said below
- memory0: float32 [8192, 256], P('dp'), may hold values from -6 to 6
- msg_weight: bfloat16 [186, 256], replicated, may hold values from -0.4375 to 0.4375
- gate_weight: bfloat16 [256, 512], replicated, may hold values from -0.375 to 0.375
- gate_bias: float32 [512], replicated, may hold values from -4 to 4
- omega: float32 [256], replicated, may hold values from 0.001 to 1
- attn_weights: bfloat16 [4, 256, 256], replicated, may hold values from -0.375 to 0.375
- pred_weights: bfloat16 [2, 256, 256], replicated, may hold values from -0.375 to 0.375
- pred_out: float32 [256], replicated, may hold values from -0.375 to 0.375
Outputs:
- scores: float32 [8, 8192], P('tm', 'dp')
- new_memory: float32 [8, 8192, 256], P('tm', 'dp')
- grad_out_proj: float32 [256, 256], replicated
- grad_pred: float32 [2, 256, 256], replicated
Inputs may be any that keep to these rules, and one draw needn't show every extreme that they name: `node_list`: each block of 32 slots (one device's requests to one owner) holds distinct rows first and 128 in the empty slots after them; every block holds at least one row; in each mini-batch some owner's block is full from every device. `endpoint_slots`: every slot points at a non-empty entry of its device's node list. `neighbor_slots`: every slot points at a non-empty entry of its device's node list.
All inputs are finite; a program needn't handle non-finite values.
Results may differ from a plain program's by a relative error of at most 0.017.
Values may be sent and summed in bfloat16 or wider, within the bound.
No kernel may reach another device: no remote copies, remote signals or barrier semaphores. Data moves between devices by JAX's collectives and lax.ppermute only.
A program may use at most 64 MiB of HBM per device.

v0:
```python
import math
import jax
import jax.numpy as jnp
from jax import lax
from jax.sharding import PartitionSpec as P

HEADS = 2


def local_step(
    slot_rows,
    end_slots,
    near_slots,
    near_gaps,
    cot_rows,
    omega,
    attn_weights,
    pred_weights,
    pred_out,
):
    feat_width = slot_rows.shape[1]
    events = end_slots.shape[1]
    near_count = near_slots.shape[0] // 2
    head_dim = feat_width // HEADS
    self_rows = jnp.take(slot_rows, end_slots, axis=0)
    near_rows = jnp.take(slot_rows, near_slots, axis=0).reshape(2, near_count, events, feat_width)
    phases = near_gaps.reshape(2, near_count, events).astype(jnp.float32)[..., None] * omega
    near_feat = (near_rows.astype(jnp.float32) + jnp.cos(phases)).astype(jnp.bfloat16)
    query_proj = jnp.einsum(
        "pea,ab->peb", self_rows, attn_weights[0], preferred_element_type=jnp.float32
    )
    key_proj = jnp.einsum(
        "pkea,ab->pkeb", near_feat, attn_weights[1], preferred_element_type=jnp.float32
    )
    value_proj = jnp.einsum(
        "pkea,ab->pkeb", near_feat, attn_weights[2], preferred_element_type=jnp.float32
    )
    query_heads = query_proj.reshape(2, 1, events, HEADS, head_dim)
    key_heads = key_proj.reshape(2, near_count, events, HEADS, head_dim)
    value_heads = value_proj.reshape(2, near_count, events, HEADS, head_dim)
    att_logits = jnp.sum(query_heads * key_heads, axis=-1) / math.sqrt(head_dim)
    weights_att = jax.nn.softmax(att_logits, axis=1)
    mixed_heads = (
        jnp.sum(weights_att[..., None] * value_heads, axis=1)
        .reshape(2, events, feat_width)
        .astype(jnp.bfloat16)
    )
    state_full = self_rows.astype(jnp.float32) + jnp.einsum(
        "pea,ab->peb", mixed_heads, attn_weights[3], preferred_element_type=jnp.float32
    )
    state_bf = state_full.astype(jnp.bfloat16)
    pre_pred = jnp.dot(state_bf[0], pred_weights[0], preferred_element_type=jnp.float32) + jnp.dot(
        state_bf[1], pred_weights[1], preferred_element_type=jnp.float32
    )
    sigmoid_pre = jax.nn.sigmoid(pre_pred)
    logit_out = jnp.sum(pre_pred * sigmoid_pre * pred_out, axis=-1)
    grad_pre = (
        cot_rows[:, None] * pred_out * (sigmoid_pre * (1.0 + pre_pred * (1.0 - sigmoid_pre)))
    ).astype(jnp.bfloat16)
    grad_first = jnp.einsum("ea,eb->ab", state_bf[0], grad_pre, preferred_element_type=jnp.float32)
    grad_second = jnp.einsum("ea,eb->ab", state_bf[1], grad_pre, preferred_element_type=jnp.float32)
    grad_state = jnp.einsum(
        "eb,pab->pea", grad_pre, pred_weights, preferred_element_type=jnp.float32
    ).astype(jnp.bfloat16)
    grad_out_proj = jnp.einsum(
        "pea,peb->ab", mixed_heads, grad_state, preferred_element_type=jnp.float32
    )
    return (logit_out, grad_out_proj, jnp.stack([grad_first, grad_second]))


def exchange(value, axis):
    return lax.all_to_all(value, axis, split_axis=0, concat_axis=0, tiled=True)


def sum_everywhere(grads):
    parts, spots = (lax.axis_size("tm"), lax.axis_size("dp"))
    rows, width = grads.shape
    own = rows // parts
    pieces = exchange(grads.astype(jnp.bfloat16).reshape(parts, own, width), "tm")
    mine = jnp.sum(pieces.astype(jnp.float32), axis=0).astype(jnp.bfloat16)
    cells = own * width // spots // 128
    pieces = exchange(mine.reshape(spots, cells, 128), "dp")
    mine = jnp.sum(pieces.astype(jnp.float32), axis=0).astype(jnp.bfloat16)
    whole = exchange(jnp.broadcast_to(mine[None], (spots, cells, 128)), "dp")
    whole = whole.reshape(own, width)
    return lax.all_gather(whole, "tm", axis=0, tiled=True).astype(jnp.float32)


def per_device(
    edge_feat,
    endpoint_slots,
    neighbor_slots,
    neighbor_gap,
    score_grad,
    node_list,
    memory0,
    msg_weight,
    gate_weight,
    gate_bias,
    omega,
    attn_weights,
    pred_weights,
    pred_out,
):
    groups = lax.axis_size("dp")
    batches = lax.axis_size("tm")
    node_dev, feat_width = memory0.shape
    list_len = node_list.shape[2]
    per_owner = list_len // groups
    requests = node_list[0, 0].reshape(groups, per_owner)
    message = jnp.dot(edge_feat[0], msg_weight, preferred_element_type=jnp.float32).astype(
        jnp.bfloat16
    )
    end_slots = endpoint_slots[0]
    slot_of = jnp.arange(list_len, dtype=jnp.int32)[:, None]
    hits = (end_slots[0][None, :] == slot_of).astype(jnp.float32) + (
        end_slots[1][None, :] == slot_of
    ).astype(jnp.float32)
    slot_tally = jnp.sum(hits, axis=1).astype(jnp.int32)
    slot_sums = jnp.dot(
        hits.astype(jnp.bfloat16), message, preferred_element_type=jnp.float32
    ).astype(jnp.bfloat16)
    small = exchange(
        jnp.concatenate([requests, slot_tally.reshape(groups, per_owner)], axis=1), "dp"
    )
    got_sums = exchange(slot_sums.reshape(groups, per_owner, feat_width), "dp")
    wanted = small[:, :per_owner].reshape(-1)
    got_tally = small[:, per_owner:].reshape(-1)
    picker = (wanted[:, None] == jnp.arange(node_dev)[None, :]).astype(jnp.bfloat16)
    totals = jnp.einsum(
        "sn,sd->nd", picker, got_sums.reshape(-1, feat_width), preferred_element_type=jnp.float32
    )
    counts = jnp.sum(
        jnp.where(wanted[:, None] == jnp.arange(node_dev)[None, :], got_tally[:, None], 0), axis=0
    ).astype(jnp.float32)
    touched = (counts > 0.5).astype(jnp.float32)
    mean_msg = (totals / jnp.maximum(counts, 1.0)[:, None]).astype(jnp.bfloat16)
    pre_gate = jnp.dot(mean_msg, gate_weight, preferred_element_type=jnp.float32) + gate_bias
    update = jax.nn.sigmoid(pre_gate[:, :feat_width]) * touched[:, None]
    candidate = jnp.tanh(pre_gate[:, feat_width:])
    decay_rate = 1.0 - update
    inject = update * candidate
    section_index = lax.axis_index("tm")
    share = node_dev // batches
    steps = exchange(
        jnp.concatenate(
            [
                decay_rate.astype(jnp.bfloat16).reshape(batches, share, feat_width),
                inject.astype(jnp.bfloat16).reshape(batches, share, feat_width),
            ],
            axis=1,
        ),
        "tm",
    ).astype(jnp.float32)
    state = lax.dynamic_slice_in_dim(memory0, section_index * share, share, axis=0)
    states = []
    for batch in range(batches):
        states.append(state.astype(jnp.bfloat16))
        state = steps[batch, :share] * state + steps[batch, share:]
    memory_bf = exchange(jnp.stack(states), "tm").reshape(node_dev, feat_width)
    before = jnp.where(section_index == 0, memory0, memory_bf.astype(jnp.float32))
    new_memory = decay_rate * before + inject
    sent_rows = jnp.dot(picker, memory_bf, preferred_element_type=jnp.float32).astype(jnp.bfloat16)
    slot_rows = exchange(sent_rows.reshape(groups, per_owner, feat_width), "dp").reshape(
        list_len, feat_width
    )
    logit_out, grad_out, grad_pair = local_step(
        slot_rows,
        end_slots,
        neighbor_slots[0],
        neighbor_gap[0],
        score_grad[0],
        omega,
        attn_weights,
        pred_weights,
        pred_out,
    )
    grads = sum_everywhere(jnp.concatenate([grad_out[None], grad_pair]).reshape(-1, feat_width))
    grads = grads.reshape(3, feat_width, feat_width)
    return (logit_out[None, :], new_memory[None], grads[0], grads[1:])


def solution(mesh):
    in_specs = (
        P("tm", "dp", None),
        P("tm", None, "dp"),
        P("tm", None, "dp"),
        P("tm", None, "dp"),
        P("tm", "dp"),
        P("tm", "dp", None),
        P("dp", None),
        P(),
        P(),
        P(),
        P(),
        P(),
        P(),
        P(),
    )
    out_specs = (P("tm", "dp"), P("tm", "dp", None), P(), P())
    return jax.shard_map(
        per_device, mesh=mesh, in_specs=in_specs, out_specs=out_specs, check_vma=False
    )
```

profile of v0, /device:TPU:1, one launch (start us, length us, event | category | flops | bytes accessed | tf_op | source)
XLA Modules:
  0.0 273.3 jit_solution(15879573352199052210)
XLA Ops:
  0.6 0.0 copy-start
  0.6 0.8 slice_bitcast_fusion.24
  1.4 0.3 fusion.8
  1.8 0.1 convert_element_type.165
  1.8 0.5 broadcast.167
  2.4 1.4 reduce.7
  3.7 0.1 reshape_squeeze.4
  3.8 0.7 pad_add_fusion
  4.5 19.3 %all-to-all-start = ((s32[64,1,64]{2,1,0:T(1,128)}), s32[64,1,64]{2,1,0:T(1,128)S(1)}, u32[]{:S(2)}, u32[]{:S(2)}) async-start(s32[64,1,64]{2,1,0:T(1,128)} %bitcast.4), calls=%async_computation | async-start | bytes 65536 | tf_op jit(solution)/shard_map/all_to_all | solution.py:72
  23.8 2.6 convolution_convert_fusion
  26.3 10.8 %all-to-all-done = s32[64,1,64]{2,1,0:T(1,128)S(1)} async-done(((s32[64,1,64]{2,1,0:T(1,128)}), s32[64,1,64]{2,1,0:T(1,128)S(1)}, u32[]{:S(2)}, u32[]{:S(2)}) %all-to-all-start) | async-done | bytes 16416 | tf_op jit(solution)/shard_map/all_to_all | solution.py:72
  37.2 4.7 %all-to-all-start.1 = ((bf16[64,32,256]{2,1,0:T(8,128)(2,1)}), bf16[64,32,256]{2,1,0:T(8,128)(2,1)S(1)}, u32[]{:S(2)}, u32[]{:S(2)}) async-start(bf16[64,32,256]{2,1,0:T(8,128)(2,1)} %bitcast.8), calls=%async_computation.1 | async-start | bytes 2097152 | tf_op jit(solution)/shard_map/all_to_all | solution.py:72
  41.8 0.1 fusion.60
  41.9 0.1 broadcast_in_dim.64
  42.0 0.1 eq.63
  42.0 1.2 select_reduce_fusion
  43.3 48.9 %all-to-all-done.1 = bf16[64,32,256]{2,1,0:T(8,128)(2,1)S(1)} async-done(((bf16[64,32,256]{2,1,0:T(8,128)(2,1)}), bf16[64,32,256]{2,1,0:T(8,128)(2,1)S(1)}, u32[]{:S(2)}, u32[]{:S(2)}) %all-to-all-start.1) | async-done | bytes 1048608 | tf_op jit(solution)/shard_map/all_to_all | solution.py:72
  92.1 0.0 copy-done
  92.1 1.0 convolution_add_fusion.1
  93.1 0.1 subtract_convert_fusion
  93.2 0.7 pad_maximum_fusion.1
  93.8 10.3 %all-to-all-start.2 = ((bf16[8,32,256]{2,1,0:T(8,128)(2,1)}), bf16[8,32,256]{2,1,0:T(8,128)(2,1)S(1)}, u32[]{:S(2)}, u32[]{:S(2)}) async-start(bf16[8,32,256]{2,1,0:T(8,128)(2,1)} %pad_maximum_fusion.1), calls=%async_computation.2 | async-start | bytes 262144 | tf_op jit(solution)/shard_map/all_to_all | solution.py:72
  104.1 5.3 %all-to-all-done.2 = bf16[8,32,256]{2,1,0:T(8,128)(2,1)S(1)} async-done(((bf16[8,32,256]{2,1,0:T(8,128)(2,1)}), bf16[8,32,256]{2,1,0:T(8,128)(2,1)S(1)}, u32[]{:S(2)}, u32[]{:S(2)}) %all-to-all-start.2) | async-done | bytes 131104 | tf_op jit(solution)/shard_map/all_to_all | solution.py:72
  109.5 8.1 %all_to_all.47 = bf16[8,16,256]{2,1,0:T(8,128)(2,1)S(1)} all-to-all(bf16[8,16,256]{2,1,0:T(8,128)(2,1)S(1)} %constant_dynamic-update-slice_fusion), channel_id=1, replica_groups=mesh['tm'=8,'dp'=64] {'tm'}, dimensions={0} | all-to-all | bytes 131072 | tf_op jit(solution)/shard_map/all_to_all | solution.py:72
  117.6 1.5 convolution_convert_fusion.1
  119.1 5.7 %all-to-all-start.4 = ((bf16[64,32,256]{2,1,0:T(8,128)(2,1)}), bf16[64,32,256]{2,1,0:T(8,128)(2,1)S(1)}, u32[]{:S(2)}, u32[]{:S(2)}) async-start(bf16[64,32,256]{2,1,0:T(8,128)(2,1)} %bitcast.34), calls=%async_computation.4 | async-start | bytes 2097152 | tf_op jit(solution)/shard_map/all_to_all | solution.py:72
  124.8 0.0 copy-start.7
  124.8 0.0 copy-start.5
  124.9 0.1 copy.42
  125.0 0.8 copy.44
  125.8 0.1 copy.45
  126.0 50.3 %all-to-all-done.4 = bf16[64,32,256]{2,1,0:T(8,128)(2,1)S(1)} async-done(((bf16[64,32,256]{2,1,0:T(8,128)(2,1)}), bf16[64,32,256]{2,1,0:T(8,128)(2,1)S(1)}, u32[]{:S(2)}, u32[]{:S(2)}) %all-to-all-start.4) | async-done | bytes 1048608 | tf_op jit(solution)/shard_map/all_to_all | solution.py:72
  176.3 1.2 gather_fusion
  177.4 0.0 copy-start.8
  177.4 7.6 %gather_fusion.1 = bf16[2560,256]{1,0:T(8,128)(2,1)S(1)} fusion(bf16[2048,256]{1,0:T(8,128)(2,1)S(1)} %bitcast.271, s32[3072]{0:T(1024)S(1)} %pad_clamp_fusion), kind=kCustom, calls=%fused_computation.1 | custom fusion | bytes 2631680 | tf_op jit(solution)/shard_map/jit(_take)/gather | solution.py:26
  185.0 0.3 fusion.20
  185.3 0.0 copy-start.4
  185.3 10.1 %add_convert_fusion = bf16[20,128,256]{2,1,0:T(8,128)(2,1)S(1)} fusion(f32[256]{0:T(256)S(1)} %copy-done.8, f32[20,128]{1,0:T(8,128)S(1)} %bitcast.289, bf16[20,128,256]{2,1,0:T(8,128)(2,1)S(1)} %bitcast.272, pred[20,128]{1,0:T(8,128)(4,1)S(1)} %compare_and_fusion), kind=kLoop, calls=%fused_computation.4 | loop fusion | flops 3276800 | bytes 2635264 | tf_op jit(solution)/shard_map/convert_element_type | solution.py:28
  195.5 0.6 multiply_reduce_fusion.1
  196.1 0.0 copy-start.1
  196.1 0.0 copy-start.10
  196.1 0.0 copy-start.11
  196.2 1.1 multiply_reduce_fusion
  197.3 0.1 copy.46
  197.4 1.1 fusion.1
  198.5 0.2 fusion.23
  198.7 0.8 multiply_convert_fusion
  199.6 0.4 fusion.5
  200.0 0.2 fusion.4
  200.2 0.2 fusion.3
  200.4 15.2 %all_to_all.48 = bf16[8,96,256]{2,1,0:T(8,128)(2,1)S(1)} all-to-all(bf16[8,96,256]{2,1,0:T(8,128)(2,1)S(1)} %bitcast.273), channel_id=1, replica_groups=mesh['tm'=8,'dp'=64] {'tm'}, dimensions={0} | all-to-all | bytes 786432 | tf_op jit(solution)/shard_map/all_to_all | solution.py:72
  215.7 0.1 reduce_sum.84
  215.7 0.7 reshape.230
  216.4 5.6 %all-to-all-start.6 = ((bf16[64,3,128]{2,1,0:T(4,128)(2,1)}), bf16[64,3,128]{2,1,0:T(4,128)(2,1)S(1)}, u32[]{:S(2)}, u32[]{:S(2)}) async-start(bf16[64,3,128]{2,1,0:T(4,128)(2,1)} %reshape.230), calls=%async_computation.6 | async-start | bytes 131072 | tf_op jit(solution)/shard_map/all_to_all | solution.py:72
  222.0 14.0 %all-to-all-done.6 = bf16[64,3,128]{2,1,0:T(4,128)(2,1)S(1)} async-done(((bf16[64,3,128]{2,1,0:T(4,128)(2,1)}), bf16[64,3,128]{2,1,0:T(4,128)(2,1)S(1)}, u32[]{:S(2)}, u32[]{:S(2)}) %all-to-all-start.6) | async-done | bytes 49184 | tf_op jit(solution)/shard_map/all_to_all | solution.py:72
  236.0 0.1 reduce_sum.85
  236.0 0.7 broadcast_in_dim.73
  236.7 4.6 %all-to-all-start.7 = ((bf16[64,3,128]{2,1,0:T(4,128)(2,1)}), bf16[64,3,128]{2,1,0:T(4,128)(2,1)S(1)}, u32[]{:S(2)}, u32[]{:S(2)}) async-start(bf16[64,3,128]{2,1,0:T(4,128)(2,1)} %broadcast_in_dim.73), calls=%async_computation.7 | async-start | bytes 131072 | tf_op jit(solution)/shard_map/all_to_all | solution.py:72
  241.3 0.8 add_bitcast_fusion
  242.1 13.3 %all-to-all-done.7 = bf16[64,3,128]{2,1,0:T(4,128)(2,1)S(1)} async-done(((bf16[64,3,128]{2,1,0:T(4,128)(2,1)}), bf16[64,3,128]{2,1,0:T(4,128)(2,1)S(1)}, u32[]{:S(2)}, u32[]{:S(2)}) %all-to-all-start.7) | async-done | bytes 49184 | tf_op jit(solution)/shard_map/all_to_all | solution.py:72
  255.3 0.1 reshape.231
  255.4 16.4 %all_gather.3 = bf16[768,256]{1,0:T(8,128)(2,1)S(1)} all-gather(bf16[96,256]{1,0:T(8,128)(2,1)S(1)} %reshape.231), channel_id=1, replica_groups=mesh['tm'=8,'dp'=64] {'tm'}, dimensions={0}, use_global_device_ids=true | all-gather | bytes 442368 | tf_op jit(solution)/shard_map/all_gather | solution.py:86
  271.8 0.7 slice.153
  272.5 0.8 slice.154
  (40 shorter events, 0.4 us)
Async XLA Ops:
  0.6 91.5 %copy-start = (bf16[256,512]{1,0:T(8,128)(2,1)S(1)}, bf16[256,512]{1,0:T(8,128)(2,1)}, u32[]{:S(2)}) copy-start(bf16[256,512]{1,0:T(8,128)(2,1)} %param.22) | copy-start | bytes 786436
  4.5 32.7 %all-to-all-start = ((s32[64,1,64]{2,1,0:T(1,128)}), s32[64,1,64]{2,1,0:T(1,128)S(1)}, u32[]{:S(2)}, u32[]{:S(2)}) async-start(s32[64,1,64]{2,1,0:T(1,128)} %bitcast.4), calls=%async_computation | async-start | bytes 65536 | tf_op jit(solution)/shard_map/all_to_all | solution.py:72
  26.3 65.8 %copy-start.9 = (f32[512]{0:T(512)S(1)}, f32[512]{0:T(512)}, u32[]{:S(2)}) copy-start(f32[512]{0:T(512)} %param.23) | copy-start | bytes 6148
  37.2 54.9 %all-to-all-start.1 = ((bf16[64,32,256]{2,1,0:T(8,128)(2,1)}), bf16[64,32,256]{2,1,0:T(8,128)(2,1)S(1)}, u32[]{:S(2)}, u32[]{:S(2)}) async-start(bf16[64,32,256]{2,1,0:T(8,128)(2,1)} %bitcast.8), calls=%async_computation.1 | async-start | bytes 2097152 | tf_op jit(solution)/shard_map/all_to_all | solution.py:72
  92.1 12.0 %copy-start.3 = (f32[128,256]{1,0:T(8,128)S(1)}, f32[128,256]{1,0:T(8,128)}, u32[]{:S(2)}) copy-start(f32[128,256]{1,0:T(8,128)} %param.20) | copy-start | bytes 393220
  93.8 15.5 %all-to-all-start.2 = ((bf16[8,32,256]{2,1,0:T(8,128)(2,1)}), bf16[8,32,256]{2,1,0:T(8,128)(2,1)S(1)}, u32[]{:S(2)}, u32[]{:S(2)}) async-start(bf16[8,32,256]{2,1,0:T(8,128)(2,1)} %pad_maximum_fusion.1), calls=%async_computation.2 | async-start | bytes 262144 | tf_op jit(solution)/shard_map/all_to_all | solution.py:72
  119.1 5.7 %copy-start.6 = (s32[1,20,128]{2,0,1:T(1,128)S(1)}, s32[1,20,128]{2,0,1:T(1,128)}, u32[]{:S(2)}) copy-start(s32[1,20,128]{2,0,1:T(1,128)} %param.17) | copy-start | bytes 30724
  119.1 5.8 %copy-start.2 = (bf16[4,256,256]{2,1,0:T(8,128)(2,1)S(1)}, bf16[4,256,256]{2,1,0:T(8,128)(2,1)}, u32[]{:S(2)}) copy-start(bf16[4,256,256]{2,1,0:T(8,128)(2,1)} %param.25) | copy-start | bytes 1572868
  119.1 57.2 %all-to-all-start.4 = ((bf16[64,32,256]{2,1,0:T(8,128)(2,1)}), bf16[64,32,256]{2,1,0:T(8,128)(2,1)S(1)}, u32[]{:S(2)}, u32[]{:S(2)}) async-start(bf16[64,32,256]{2,1,0:T(8,128)(2,1)} %bitcast.34), calls=%async_computation.4 | async-start | bytes 2097152 | tf_op jit(solution)/shard_map/all_to_all | solution.py:72
  124.8 1.1 copy-start.7
  124.8 1.1 copy-start.5
  177.4 7.9 %copy-start.8 = (f32[256]{0:T(256)S(1)}, f32[256]{0:T(256)}, u32[]{:S(2)}) copy-start(f32[256]{0:T(256)} %param.24) | copy-start | bytes 3076
  185.3 10.1 %copy-start.4 = (bf16[256,256]{1,0:T(8,128)(2,1)S(1)}, bf16[256,256]{1,0:T(8,128)(2,1)}, u32[]{:S(2)}) copy-start(bf16[256,256]{1,0:T(8,128)(2,1)} %copy.44) | copy-start | bytes 393220
  196.1 2.4 copy-start.1
  196.1 2.6 copy-start.10
  196.1 2.6 copy-start.11
  216.4 19.6 %all-to-all-start.6 = ((bf16[64,3,128]{2,1,0:T(4,128)(2,1)}), bf16[64,3,128]{2,1,0:T(4,128)(2,1)S(1)}, u32[]{:S(2)}, u32[]{:S(2)}) async-start(bf16[64,3,128]{2,1,0:T(4,128)(2,1)} %reshape.230), calls=%async_computation.6 | async-start | bytes 131072 | tf_op jit(solution)/shard_map/all_to_all | solution.py:72
  236.7 18.6 %all-to-all-start.7 = ((bf16[64,3,128]{2,1,0:T(4,128)(2,1)}), bf16[64,3,128]{2,1,0:T(4,128)(2,1)S(1)}, u32[]{:S(2)}, u32[]{:S(2)}) async-start(bf16[64,3,128]{2,1,0:T(4,128)(2,1)} %broadcast_in_dim.73), calls=%async_computation.7 | async-start | bytes 131072 | tf_op jit(solution)/shard_map/all_to_all | solution.py:72
where the time goes:
time: 274 us; the launch traced here: 273 us
  waiting for transfers between devices  142 us (52%)
  starting transfers between devices  50.1 us (18%)
  blocking collectives  39.7 us (14%)
  other arithmetic  15.7 us (6%)
  local copies, waits for them, and re-layouts  14.5 us (5%)
  matrix products  9.86 us (4%)
    all_to_all x6, waiting for transfers between devices, exchange(): return lax.all_to_all(value, axis, split_axis=0, concat_axis=0, tiled=True)  142 us
    all_to_all x6, starting transfers between devices, exchange(): return lax.all_to_all(value, axis, split_axis=0, concat_axis=0, tiled=True)  50.1 us
    all_to_all x2, blocking collectives, exchange(): return lax.all_to_all(value, axis, split_axis=0, concat_axis=0, tiled=True)  23.3 us
    all_gather x1, blocking collectives, sum_everywhere(): return lax.all_gather(whole, 'tm', axis=0, tiled=True).astype(jnp.float32)  16.4 us
    convert_element_type x1, other arithmetic, local_step(): (near_rows.astype(jnp.float32) + jnp.cos(phases)).astype(jnp.bfloat16)  10.1 us
    gather x1, local copies, waits for them, and re-layouts, local_step(): jnp.take(slot_rows, near_slots, axis=0)  7.57 us
  transfers between devices with their start and end apart: 6, of which 6 were waited for; matrix products, arithmetic and copies ran while one was open for 2% of the time, Pallas kernels for 0%

commit v1 on v0

--- a/solution.py
+++ b/solution.py
@@ -5,6 +5,11 @@
 from jax.sharding import PartitionSpec as P
 
 HEADS = 2
+
+
+def gather_by_exchange(shard, axis, dim):
+    copies = jnp.concatenate([shard] * lax.axis_size(axis), axis=dim)
+    return lax.all_to_all(copies, axis, dim, dim, tiled=True)
 
 
 def local_step(
@@ -83,7 +88,7 @@
     mine = jnp.sum(pieces.astype(jnp.float32), axis=0).astype(jnp.bfloat16)
     whole = exchange(jnp.broadcast_to(mine[None], (spots, cells, 128)), "dp")
     whole = whole.reshape(own, width)
-    return lax.all_gather(whole, "tm", axis=0, tiled=True).astype(jnp.float32)
+    return gather_by_exchange(whole, "tm", 0).astype(jnp.float32)
 
 
 def per_device(

time: 274 us -> 276 us (level)
  blocking collectives: 39.7 us -> 60.5 us
  waiting for transfers between devices: 142 us -> 123 us
  local copies, waits for them, and re-layouts: 14.5 us -> 18.2 us
  starting transfers between devices: 50.1 us -> 46.8 us
    all_to_all x2 -> x4, blocking collectives: 23.3 us -> 60.5 us  [exchange(): return lax.all_to_all(value, axis, split_axis=0, concat_axis=0, tiled=True)]
    all_to_all x6 -> x4, waiting for transfers between devices: 142 us -> 115 us  [exchange(): return lax.all_to_all(value, axis, split_axis=0, concat_axis=0, tiled=True)]
    all_gather x1 -> x0, blocking collectives: 16.4 us -> none  [sum_everywhere(): return lax.all_gather(whole, 'tm', axis=0, tiled=True).astype(jnp.float32)]
    all_to_all x6 -> x4, starting transfers between devices: 50.1 us -> 39.9 us  [exchange(): return lax.all_to_all(value, axis, split_axis=0, concat_axis=0, tiled=True)]
    all_to_all x0 -> x1, waiting for transfers between devices: none -> 7.35 us  [gather_by_exchange(): return lax.all_to_all(copies, axis, dim, dim, tiled=True)]
    all_to_all x0 -> x1, starting transfers between devices: none -> 6.92 us  [gather_by_exchange(): return lax.all_to_all(copies, axis, dim, dim, tiled=True)]
    unnamed x27 -> x34, local copies, waits for them, and re-layouts: 0.59 us -> 4.95 us
  transfers between devices with their start and end apart: 6 -> 5, of which waited for: 6 -> 5; matrix products, arithmetic and copies ran while one was open for 2% -> 2% of each run, Pallas kernels for 0% -> 0%
where the time goes in v1:
time: 276 us; the launch traced here: 275 us
  waiting for transfers between devices  123 us (45%)
  blocking collectives  60.5 us (22%)
  starting transfers between devices  46.8 us (17%)
  local copies, waits for them, and re-layouts  18.2 us (7%)
  other arithmetic  15.7 us (6%)
  matrix products  9.85 us (4%)
    all_to_all x4, waiting for transfers between devices, exchange(): return lax.all_to_all(value, axis, split_axis=0, concat_axis=0, tiled=True)  115 us
    all_to_all x4, blocking collectives, exchange(): return lax.all_to_all(value, axis, split_axis=0, concat_axis=0, tiled=True)  60.5 us
    all_to_all x4, starting transfers between devices, exchange(): return lax.all_to_all(value, axis, split_axis=0, concat_axis=0, tiled=True)  39.9 us
    convert_element_type x1, other arithmetic, local_step(): (near_rows.astype(jnp.float32) + jnp.cos(phases)).astype(jnp.bfloat16)  10.1 us
    gather x1, local copies, waits for them, and re-layouts, local_step(): jnp.take(slot_rows, near_slots, axis=0)  7.57 us
    all_to_all x1, waiting for transfers between devices, gather_by_exchange(): return lax.all_to_all(copies, axis, dim, dim, tiled=True)  7.35 us
    all_to_all x1, starting transfers between devices, gather_by_exchange(): return lax.all_to_all(copies, axis, dim, dim, tiled=True)  6.92 us
  transfers between devices with their start and end apart: 5, of which 5 were waited for; matrix products, arithmetic and copies ran while one was open for 2% of the time, Pallas kernels for 0%

profile of v1, /device:TPU:1, one launch (start us, length us, event | category | flops | bytes accessed | tf_op | source)
XLA Modules:
  0.0 274.8 jit_solution(8383268286700365743)
XLA Ops:
  0.6 0.0 copy-start
  0.6 0.8 slice_bitcast_fusion.24
  1.4 0.3 fusion.8
  1.8 0.1 convert_element_type.168
  1.8 0.5 broadcast.167
  2.4 1.4 reduce.7
  3.7 0.1 reshape_squeeze.4
  3.8 0.7 pad_add_fusion
  4.5 19.3 %all-to-all-start = ((s32[64,1,64]{2,1,0:T(1,128)}), s32[64,1,64]{2,1,0:T(1,128)S(1)}, u32[]{:S(2)}, u32[]{:S(2)}) async-start(s32[64,1,64]{2,1,0:T(1,128)} %bitcast.4), calls=%async_computation | async-start | bytes 65536 | tf_op jit(solution)/shard_map/all_to_all | solution.py:77
  23.8 2.6 convolution_convert_fusion
  26.3 10.8 %all-to-all-done = s32[64,1,64]{2,1,0:T(1,128)S(1)} async-done(((s32[64,1,64]{2,1,0:T(1,128)}), s32[64,1,64]{2,1,0:T(1,128)S(1)}, u32[]{:S(2)}, u32[]{:S(2)}) %all-to-all-start) | async-done | bytes 16416 | tf_op jit(solution)/shard_map/all_to_all | solution.py:77
  37.2 4.7 %all-to-all-start.1 = ((bf16[64,32,256]{2,1,0:T(8,128)(2,1)}), bf16[64,32,256]{2,1,0:T(8,128)(2,1)S(1)}, u32[]{:S(2)}, u32[]{:S(2)}) async-start(bf16[64,32,256]{2,1,0:T(8,128)(2,1)} %bitcast.8), calls=%async_computation.1 | async-start | bytes 2097152 | tf_op jit(solution)/shard_map/all_to_all | solution.py:77
  41.8 0.1 fusion.60
  41.9 0.1 broadcast_in_dim.64
  42.0 0.1 eq.63
  42.0 1.2 select_reduce_fusion
  43.3 48.9 %all-to-all-done.1 = bf16[64,32,256]{2,1,0:T(8,128)(2,1)S(1)} async-done(((bf16[64,32,256]{2,1,0:T(8,128)(2,1)}), bf16[64,32,256]{2,1,0:T(8,128)(2,1)S(1)}, u32[]{:S(2)}, u32[]{:S(2)}) %all-to-all-start.1) | async-done | bytes 1048608 | tf_op jit(solution)/shard_map/all_to_all | solution.py:77
  92.1 1.0 convolution_add_fusion.1
  93.1 0.1 subtract_convert_fusion
  93.2 0.7 pad_maximum_fusion.1
  93.8 10.3 %all-to-all-start.2 = ((bf16[8,32,256]{2,1,0:T(8,128)(2,1)}), bf16[8,32,256]{2,1,0:T(8,128)(2,1)S(1)}, u32[]{:S(2)}, u32[]{:S(2)}) async-start(bf16[8,32,256]{2,1,0:T(8,128)(2,1)} %pad_maximum_fusion.1), calls=%async_computation.2 | async-start | bytes 262144 | tf_op jit(solution)/shard_map/all_to_all | solution.py:77
  104.1 5.3 %all-to-all-done.2 = bf16[8,32,256]{2,1,0:T(8,128)(2,1)S(1)} async-done(((bf16[8,32,256]{2,1,0:T(8,128)(2,1)}), bf16[8,32,256]{2,1,0:T(8,128)(2,1)S(1)}, u32[]{:S(2)}, u32[]{:S(2)}) %all-to-all-start.2) | async-done | bytes 131104 | tf_op jit(solution)/shard_map/all_to_all | solution.py:77
  109.5 8.1 %all_to_all.56 = bf16[8,16,256]{2,1,0:T(8,128)(2,1)S(1)} all-to-all(bf16[8,16,256]{2,1,0:T(8,128)(2,1)S(1)} %constant_dynamic-update-slice_fusion), channel_id=1, replica_groups=mesh['tm'=8,'dp'=64] {'tm'}, dimensions={0} | all-to-all | bytes 131072 | tf_op jit(solution)/shard_map/all_to_all | solution.py:77
  117.6 1.5 convolution_convert_fusion.1
  119.1 5.7 %all-to-all-start.4 = ((bf16[64,32,256]{2,1,0:T(8,128)(2,1)}), bf16[64,32,256]{2,1,0:T(8,128)(2,1)S(1)}, u32[]{:S(2)}, u32[]{:S(2)}) async-start(bf16[64,32,256]{2,1,0:T(8,128)(2,1)} %bitcast.34), calls=%async_computation.4 | async-start | bytes 2097152 | tf_op jit(solution)/shard_map/all_to_all | solution.py:77
  124.8 0.0 copy-start.7
  124.9 0.1 copy.42
  125.0 0.8 copy.44
  125.8 0.1 copy.45
  126.0 50.3 %all-to-all-done.4 = bf16[64,32,256]{2,1,0:T(8,128)(2,1)S(1)} async-done(((bf16[64,32,256]{2,1,0:T(8,128)(2,1)}), bf16[64,32,256]{2,1,0:T(8,128)(2,1)S(1)}, u32[]{:S(2)}, u32[]{:S(2)}) %all-to-all-start.4) | async-done | bytes 1048608 | tf_op jit(solution)/shard_map/all_to_all | solution.py:77
  176.3 1.2 gather_fusion
  177.4 7.6 %gather_fusion.1 = bf16[2560,256]{1,0:T(8,128)(2,1)S(1)} fusion(bf16[2048,256]{1,0:T(8,128)(2,1)S(1)} %bitcast.275, s32[3072]{0:T(1024)S(1)} %pad_clamp_fusion), kind=kCustom, calls=%fused_computation.1 | custom fusion | bytes 2631680 | tf_op jit(solution)/shard_map/jit(_take)/gather | solution.py:31
  185.0 0.3 fusion.20
  185.3 10.1 %add_convert_fusion = bf16[20,128,256]{2,1,0:T(8,128)(2,1)S(1)} fusion(f32[256]{0:T(256)S(1)} %copy-done.8, f32[20,128]{1,0:T(8,128)S(1)} %bitcast.293, bf16[20,128,256]{2,1,0:T(8,128)(2,1)S(1)} %bitcast.276, pred[20,128]{1,0:T(8,128)(4,1)S(1)} %compare_and_fusion), kind=kLoop, calls=%fused_computation.4 | loop fusion | flops 3276800 | bytes 2635264 | tf_op jit(solution)/shard_map/convert_element_type | solution.py:33
  195.5 0.6 multiply_reduce_fusion.1
  196.1 0.0 copy-start.1
  196.2 1.1 multiply_reduce_fusion
  197.3 0.1 copy.46
  197.4 1.1 fusion.1
  198.5 0.2 fusion.23
  198.7 0.8 multiply_convert_fusion
  199.5 0.4 fusion.5
  199.9 0.2 fusion.4
  200.2 0.2 fusion.3
  200.4 15.2 %all_to_all.57 = bf16[8,96,256]{2,1,0:T(8,128)(2,1)S(1)} all-to-all(bf16[8,96,256]{2,1,0:T(8,128)(2,1)S(1)} %bitcast.277), channel_id=1, replica_groups=mesh['tm'=8,'dp'=64] {'tm'}, dimensions={0} | all-to-all | bytes 786432 | tf_op jit(solution)/shard_map/all_to_all | solution.py:77
  215.7 0.1 reduce_sum.84
  215.8 19.4 %all_to_all.58 = bf16[64,3,128]{2,1,0:T(4,128)(2,1)S(1)} all-to-all(bf16[64,3,128]{2,1,0:T(4,128)(2,1)S(1)} %reshape.234), channel_id=1, replica_groups=mesh['tm'=8,'dp'=64] {'dp'}, dimensions={0} | all-to-all | bytes 98304 | tf_op jit(solution)/shard_map/all_to_all | solution.py:77
  235.1 0.1 reduce_sum.85
  235.2 17.8 %all_to_all.59 = bf16[64,3,128]{2,1,0:T(4,128)(2,1)S(1)} all-to-all(bf16[64,3,128]{2,1,0:T(4,128)(2,1)S(1)} %broadcast_in_dim.73), channel_id=1, replica_groups=mesh['tm'=8,'dp'=64] {'dp'}, dimensions={0} | all-to-all | bytes 98304 | tf_op jit(solution)/shard_map/all_to_all | solution.py:77
  253.0 0.1 reshape.235
  253.1 0.6 constant_dynamic-update-slice_fusion.15
  253.7 0.6 constant_dynamic-update-slice_fusion.14
  254.4 0.6 constant_dynamic-update-slice_fusion.13
  255.0 0.6 constant_dynamic-update-slice_fusion.12
  255.6 0.6 constant_dynamic-update-slice_fusion.11
  256.2 0.6 constant_dynamic-update-slice_fusion.10
  256.9 0.6 constant_dynamic-update-slice_fusion.9
  257.5 0.6 constant_dynamic-update-slice_fusion.8
  258.1 6.9 %all-to-all-start.8 = ((bf16[8,96,256]{2,1,0:T(8,128)(2,1)}), bf16[8,96,256]{2,1,0:T(8,128)(2,1)S(1)}, u32[]{:S(2)}, u32[]{:S(2)}) async-start(bf16[8,96,256]{2,1,0:T(8,128)(2,1)} %bitcast.79), calls=%async_computation.8 | async-start | bytes 786432 | tf_op jit(solution)/shard_map/all_to_all | solution.py:12
  265.0 0.7 add_bitcast_fusion
  265.8 7.3 %all-to-all-done.8 = bf16[8,96,256]{2,1,0:T(8,128)(2,1)S(1)} async-done(((bf16[8,96,256]{2,1,0:T(8,128)(2,1)}), bf16[8,96,256]{2,1,0:T(8,128)(2,1)S(1)}, u32[]{:S(2)}, u32[]{:S(2)}) %all-to-all-start.8) | async-done | bytes 393248 | tf_op jit(solution)/shard_map/all_to_all | solution.py:12
  273.1 0.1 bitcast_convert_fusion
  273.2 0.7 slice.153
  273.9 0.8 slice.154
  (48 shorter events, 0.5 us)
Async XLA Ops:
  0.6 91.5 %copy-start = (bf16[256,512]{1,0:T(8,128)(2,1)S(1)}, bf16[256,512]{1,0:T(8,128)(2,1)}, u32[]{:S(2)}) copy-start(bf16[256,512]{1,0:T(8,128)(2,1)} %param.22) | copy-start | bytes 786436
  4.5 32.7 %all-to-all-start = ((s32[64,1,64]{2,1,0:T(1,128)}), s32[64,1,64]{2,1,0:T(1,128)S(1)}, u32[]{:S(2)}, u32[]{:S(2)}) async-start(s32[64,1,64]{2,1,0:T(1,128)} %bitcast.4), calls=%async_computation | async-start | bytes 65536 | tf_op jit(solution)/shard_map/all_to_all | solution.py:77
  26.3 65.8 %copy-start.9 = (f32[512]{0:T(512)S(1)}, f32[512]{0:T(512)}, u32[]{:S(2)}) copy-start(f32[512]{0:T(512)} %param.23) | copy-start | bytes 6148
  37.2 54.9 %all-to-all-start.1 = ((bf16[64,32,256]{2,1,0:T(8,128)(2,1)}), bf16[64,32,256]{2,1,0:T(8,128)(2,1)S(1)}, u32[]{:S(2)}, u32[]{:S(2)}) async-start(bf16[64,32,256]{2,1,0:T(8,128)(2,1)} %bitcast.8), calls=%async_computation.1 | async-start | bytes 2097152 | tf_op jit(solution)/shard_map/all_to_all | solution.py:77
  92.1 12.0 %copy-start.3 = (f32[128,256]{1,0:T(8,128)S(1)}, f32[128,256]{1,0:T(8,128)}, u32[]{:S(2)}) copy-start(f32[128,256]{1,0:T(8,128)} %param.20) | copy-start | bytes 393220
  93.8 15.5 %all-to-all-start.2 = ((bf16[8,32,256]{2,1,0:T(8,128)(2,1)}), bf16[8,32,256]{2,1,0:T(8,128)(2,1)S(1)}, u32[]{:S(2)}, u32[]{:S(2)}) async-start(bf16[8,32,256]{2,1,0:T(8,128)(2,1)} %pad_maximum_fusion.1), calls=%async_computation.2 | async-start | bytes 262144 | tf_op jit(solution)/shard_map/all_to_all | solution.py:77
  119.1 5.7 %copy-start.6 = (s32[1,20,128]{2,0,1:T(1,128)S(1)}, s32[1,20,128]{2,0,1:T(1,128)}, u32[]{:S(2)}) copy-start(s32[1,20,128]{2,0,1:T(1,128)} %param.17) | copy-start | bytes 30724
  119.1 5.8 %copy-start.2 = (bf16[4,256,256]{2,1,0:T(8,128)(2,1)S(1)}, bf16[4,256,256]{2,1,0:T(8,128)(2,1)}, u32[]{:S(2)}) copy-start(bf16[4,256,256]{2,1,0:T(8,128)(2,1)} %param.25) | copy-start | bytes 1572868
  119.1 57.2 %all-to-all-start.4 = ((bf16[64,32,256]{2,1,0:T(8,128)(2,1)}), bf16[64,32,256]{2,1,0:T(8,128)(2,1)S(1)}, u32[]{:S(2)}, u32[]{:S(2)}) async-start(bf16[64,32,256]{2,1,0:T(8,128)(2,1)} %bitcast.34), calls=%async_computation.4 | async-start | bytes 2097152 | tf_op jit(solution)/shard_map/all_to_all | solution.py:77
  124.8 1.1 copy-start.7
  124.8 1.1 copy-start.5
  177.4 7.9 %copy-start.8 = (f32[256]{0:T(256)S(1)}, f32[256]{0:T(256)}, u32[]{:S(2)}) copy-start(f32[256]{0:T(256)} %param.24) | copy-start | bytes 3076
  185.3 10.1 %copy-start.4 = (bf16[256,256]{1,0:T(8,128)(2,1)S(1)}, bf16[256,256]{1,0:T(8,128)(2,1)}, u32[]{:S(2)}) copy-start(bf16[256,256]{1,0:T(8,128)(2,1)} %copy.44) | copy-start | bytes 393220
  196.1 2.4 copy-start.1
  196.1 2.6 copy-start.10
  196.1 2.6 copy-start.11
  258.1 15.0 %all-to-all-start.8 = ((bf16[8,96,256]{2,1,0:T(8,128)(2,1)}), bf16[8,96,256]{2,1,0:T(8,128)(2,1)S(1)}, u32[]{:S(2)}, u32[]{:S(2)}) async-start(bf16[8,96,256]{2,1,0:T(8,128)(2,1)} %bitcast.79), calls=%async_computation.8 | async-start | bytes 786432 | tf_op jit(solution)/shard_map/all_to_all | solution.py:12
